TPU v7x, 32 devices: a whole 2x2x4 slice. The times are simulated.
32 devices in a mesh: wide: 8 (over z, y), narrow: 4 (over x, core).
Axes of the slice: x: 2, y: 2, z: 4, core: 2. Of those that a mesh axis runs over, the one named last changes fastest.
Arguments:
- entry_factor: bfloat16 [288, 4, 64, 1024], P('wide', 'narrow'), may hold values from -6 to 6
- entry_panel: int32 [288, 4], P('wide', 'narrow'), may hold values from 0 to 1
- entry_target: int32 [288, 4], P('wide', 'narrow'), may hold values from 0 to 7, as said below
- entry_count: int32 [4, 8], P('narrow', 'wide'), may hold values from 1 to 36, 96 in all within a row
- panel_shared: bfloat16 [16, 64, 1024], P('wide', None, 'narrow'), may hold values from -0.1875 to 0.1875
- coupling: float32 [16, 64, 64], P('wide'), may hold values from -0.75 to 0.75
- probes: bfloat16 [32, 64, 1024], P('narrow'), may hold values from -6 to 6
Outputs:
- left_factor: float32 [32, 64, 1024], P('narrow', None, 'wide')
- right_factor: float32 [32, 64, 1024], P('narrow', None, 'wide')
Inputs may be any that keep to these rules, and one draw needn't show every extreme that they name: `entry_panel`: the local panel of an entry of any slot, live or not. `entry_target`: the local target of an entry; every target has at least one live entry. `entry_count`: the live slots of one device; for every owner the counts over the 8 wide indices sum to 96, and some device holds exactly 36.
All inputs are finite; a program needn't handle non-finite values.
Results may differ from a plain program's by a relative error of at most 0.0036.
Values may be sent and summed in bfloat16 or wider, within the bound.
A program may use at most 64 MiB of HBM per device.

v0:
```python
import math
import jax
import jax.numpy as jnp
from jax import lax
from jax.sharding import PartitionSpec as P


def shards(entry_factor, entry_panel, entry_target, entry_count, panel_shared, coupling, probes):
    highest = lax.Precision.HIGHEST
    factors = entry_factor[:, 0]
    slot_count = factors.shape[0]
    rank_dim = factors.shape[1]
    full_width = factors.shape[2]
    panel_count = panel_shared.shape[0]
    target_count = probes.shape[0]
    live_mask = (jnp.arange(slot_count) < entry_count[0, 0]).astype(jnp.float32)
    pick_panel = (entry_panel == jnp.arange(panel_count)[None, :]).astype(jnp.float32) * live_mask[
        :, None
    ]
    pick_target = (entry_target == jnp.arange(target_count)[None, :]).astype(jnp.float32)
    pair_pick = (pick_panel[:, :, None] * pick_target[:, None, :]).reshape(
        slot_count, panel_count * target_count
    )
    gathered = lax.all_gather(panel_shared, "narrow", axis=2, tiled=True)
    projected = jnp.einsum("drb,tkb->dtrk", gathered, probes, preferred_element_type=jnp.float32)
    coefficients = jnp.einsum("dij,dtjk->dtik", coupling, projected, precision=highest).astype(
        jnp.bfloat16
    )
    coeff_table = coefficients.reshape(panel_count * target_count, rank_dim * rank_dim)
    chosen = jnp.dot(
        pair_pick.astype(jnp.bfloat16), coeff_table, preferred_element_type=jnp.float32
    )
    chosen = chosen.astype(jnp.bfloat16).reshape(slot_count, rank_dim, rank_dim)
    contributions = jnp.einsum("eji,ejb->eib", chosen, factors, preferred_element_type=jnp.float32)
    sketch = jnp.einsum("et,eib->tib", pick_target, contributions, precision=highest)
    wide_count = lax.axis_size("wide")
    share_cols = full_width // wide_count
    sketch_part = lax.psum_scatter(sketch, "wide", scatter_dimension=2, tiled=True)
    gram_part = jnp.einsum("tib,tjb->tij", sketch_part, sketch_part, precision=highest)
    gram_matrix = lax.psum(gram_part, "wide")
    lower_factor = jnp.linalg.cholesky(gram_matrix)
    own_basis = jax.scipy.linalg.solve_triangular(lower_factor, sketch_part, lower=True)
    basis_round = lax.all_gather(own_basis.astype(jnp.bfloat16), "wide", axis=2, tiled=True)
    selected = jnp.einsum(
        "et,tkb->ekb",
        pick_target.astype(jnp.bfloat16),
        basis_round,
        preferred_element_type=jnp.float32,
    )
    selected = selected.astype(jnp.bfloat16)
    back_terms = jnp.einsum("eib,ekb->eik", factors, selected, preferred_element_type=jnp.float32)
    summed = jnp.einsum("ep,eik->pik", pair_pick, back_terms, precision=highest)
    summed = summed.reshape(panel_count, target_count, rank_dim, rank_dim)
    middle_terms = jnp.einsum("dtik,dij->dtkj", summed, coupling, precision=highest)
    partial_rows = jnp.einsum(
        "dtkj,djb->tkb", middle_terms, gathered.astype(jnp.float32), precision=highest
    )
    coeff_part = lax.psum_scatter(partial_rows, "wide", scatter_dimension=2, tiled=True)
    root_width = math.sqrt(full_width)
    return (own_basis * root_width, coeff_part / root_width)


def solution(mesh):
    placed = (
        P("wide", "narrow", None, None),
        P("wide", "narrow"),
        P("wide", "narrow"),
        P("narrow", "wide"),
        P("wide", None, "narrow"),
        P("wide", None, None),
        P("narrow", None, None),
    )
    return jax.shard_map(
        shards,
        mesh=mesh,
        in_specs=placed,
        out_specs=(P("narrow", None, "wide"), P("narrow", None, "wide")),
        check_vma=False,
    )
```

profile of v0, /device:TPU:0, one launch (start us, length us, event | category | flops | bytes accessed | tf_op | source)
XLA Modules:
  0.0 399.1 jit_solution(11624132694384365650)
XLA Ops:
  7.2 0.0 copy-start
  7.2 0.0 reduce-scatter.3.cloned.1.call-start
  7.2 0.7 fusion.36
  8.0 7.4 %all_gather.6 = bf16[2,64,1024]{2,1,0:T(8,128)(2,1)S(1)} all-gather(bf16[2,64,256]{2,1,0:T(8,128)(2,1)} %param.11), channel_id=1, replica_groups=mesh['wide'=8,'narrow'=4] {'narrow'}, dimensions={2}, use_global_device_ids=true | all-gather | bytes 327680 | tf_op jit(solution)/shard_map/all_gather | solution.py:24
  15.4 0.0 copy-done
  15.4 0.0 copy-start.1
  15.4 0.5 convolution_bitcast_fusion.1
  15.9 0.3 copy-done.1
  16.1 1.4 fusion.14
  17.6 0.2 copy.23
  17.7 0.3 reshape.98
  18.7 0.7 compare_select_fusion
  19.3 0.3 convolution_convert_fusion
  19.6 0.6 reshape.99
  20.3 0.0 copy-start.2
  20.3 3.8 fusion.4
  24.0 0.0 copy-done.2
  24.1 10.1 %fusion = f32[8,64,1024]{2,0,1:T(8,128)} fusion(f32[36,64,1024]{2,1,0:T(8,128)S(1)} %fusion.4, s32[36]{0:T(128)S(1)} %bitcast.78), kind=kOutput, calls=%fused_computation | convolution fusion | flops 226492704 | bytes 11534480 | tf_op jit(solution)/shard_map/et,eib->tib/dot_general | solution.py:35
  34.2 0.0 reduce-scatter.3.cloned.1.call-update
  34.2 0.0 all-reduce.2.cloned.1.call-start
  34.3 70.3 %reduce-scatter.3.cloned.1.call-done = f32[8,64,128]{2,0,1:T(8,128)} async-done(((f32[8,64,1024]{2,0,1:T(8,128)}), f32[8,64,128]{2,0,1:T(8,128)}) %reduce-scatter.3.cloned.1.call-update) | async-done | bytes 262160 | tf_op jit(solution)/shard_map/reduce_scatter | solution.py:38
  104.5 2.3 fusion.25
  106.8 0.0 all-reduce.2.cloned.1.call-update
  106.9 0.0 all-gather.2.cloned.1.call-start
  106.9 71.6 %all-reduce.2.cloned.1.call-done = f32[8,64,64]{1,2,0:T(8,128)} async-done(((f32[8,64,64]{1,2,0:T(8,128)}), f32[8,64,64]{1,2,0:T(8,128)}) %all-reduce.2.cloned.1.call-update) | async-done | bytes 131088 | tf_op jit(solution)/shard_map/psum | solution.py:40
  178.5 1.1 copy.29
  179.6 1.0 fusion.22
  180.6 46.9 %custom-call.8 = f32[8,64,64]{2,1,0:T(8,128)S(1)} custom-call(f32[8,64,64]{2,1,0:T(8,128)S(1)} %fusion.22), custom_call_target="Cholesky" | custom-call | tf_op jit(solution)/shard_map/jit(cholesky)/cholesky | solution.py:41
  227.5 0.1 compare_reduce_fusion
  227.6 0.1 select_bitcast_fusion
  227.8 39.3 %custom-call.9 = f32[8,1,64,64]{2,3,1,0:T(8,128)S(1)} custom-call(f32[8,1,64,64]{3,2,1,0:T(8,128)S(1)} %select_bitcast_fusion), custom_call_target="InvertDiagBlocksLowerTriangular" | custom-call | tf_op jit(solution)/shard_map/jit(_solve_triangular)/vmap()/triangular_solve | solution.py:42
  267.1 2.3 fusion.42
  269.4 0.0 all-gather.2.cloned.1.call-update
  269.4 0.0 reduce-scatter.5.cloned.1.call-start
  269.5 38.7 %all-gather.2.cloned.1.call-done = bf16[8,64,1024]{2,1,0:T(8,128)(2,1)} async-done(((bf16[8,64,128]{2,1,0:T(8,128)(2,1)}), bf16[8,64,1024]{2,1,0:T(8,128)(2,1)}) %all-gather.2.cloned.1.call-update) | async-done | bytes 1048592 | tf_op jit(solution)/shard_map/all_gather | solution.py:43
  308.2 2.8 convolution_convert_fusion.1
  311.0 5.5 %fusion.7 = f32[36,64,64]{1,2,0:T(8,128)S(1)} fusion(bf16[36,1,64,1024]{3,2,1,0:T(8,128)(2,1)} %param.7, bf16[36,64,1024]{2,0,1:T(8,128)(2,1)S(1)} %convolution_convert_fusion.1), kind=kOutput, calls=%fused_computation.10 | convolution fusion | flops 301989888 | bytes 10027008 | tf_op jit(solution)/shard_map/eib,ekb->eik/dot_general | solution.py:51
  316.4 0.5 copy.34
  316.9 0.8 fusion.12
  317.7 1.8 fusion.17
  319.5 3.3 convolution_bitcast_fusion
  322.9 0.0 reduce-scatter.5.cloned.1.call-update
  322.9 68.0 %reduce-scatter.5.cloned.1.call-done = f32[8,64,128]{2,1,0:T(8,128)} async-done(((f32[8,64,1024]{2,1,0:T(8,128)}), f32[8,64,128]{2,1,0:T(8,128)}) %reduce-scatter.5.cloned.1.call-update) | async-done | bytes 262160 | tf_op jit(solution)/shard_map/reduce_scatter | solution.py:58
  390.9 1.7 broadcast_multiply_fusion
  (4 shorter events, 0.1 us)
Async XLA Ops:
  7.2 8.2 %copy-start = (bf16[8,64,1024]{2,1,0:T(8,128)(2,1)S(1)}, bf16[8,64,1024]{2,1,0:T(8,128)(2,1)}, u32[]{:S(2)}) copy-start(bf16[8,64,1024]{2,1,0:T(8,128)(2,1)} %param.13) | copy-start | bytes 3145732
  7.2 97.3 %reduce-scatter.3.cloned.1.call-start = ((), (), s32[]{:S(2)}) async-start(), calls=%async_computation.2 | async-start | bytes 2359296 | tf_op jit(solution)/shard_map/reduce_scatter | solution.py:38
  15.4 0.7 copy-start.1
  20.3 3.8 copy-start.2
  34.2 144.3 %all-reduce.2.cloned.1.call-start = ((), (), s32[]{:S(2)}) async-start(), calls=%async_computation.3 | async-start | bytes 524288 | tf_op jit(solution)/shard_map/psum | solution.py:40
  106.9 201.3 %all-gather.2.cloned.1.call-start = ((), (), s32[]{:S(2)}) async-start(), calls=%async_computation.4 | async-start | bytes 1179648 | tf_op jit(solution)/shard_map/all_gather | solution.py:43
  269.4 121.5 %reduce-scatter.5.cloned.1.call-start = ((), (), s32[]{:S(2)}) async-start(), calls=%async_computation.5 | async-start | bytes 2359296 | tf_op jit(solution)/shard_map/reduce_scatter | solution.py:58
Sparse Core Ops, SparseCore 0:
  34.3 70.1 reduce-scatter.2
  108.4 70.0 all-reduce.1
  269.5 38.5 all-gather.1
  323.0 67.8 reduce-scatter.4
where the time goes:
time: 400 us; the launch traced here: 399 us
  waiting for transfers between devices  249 us (62%)
  other arithmetic  90.6 us (23%)
  matrix products  34.9 us (9%)
  between operations  14.6 us (4%)
  blocking collectives  7.42 us (2%)
    psum x1, waiting for transfers between devices, shards(): gram_matrix = lax.psum(gram_part, 'wide')  71.6 us
    reduce_scatter x1, waiting for transfers between devices, shards(): lax.psum_scatter(sketch, 'wide', scatter_dimension=2, tiled=True)  70.3 us
    reduce_scatter x1, waiting for transfers between devices, shards(): lax.psum_scatter(partial_rows, 'wide', scatter_dimension=2, tiled=True)  68 us
    another operation x4, other arithmetic, shards(): lower_factor = jnp.linalg.cholesky(gram_matrix)  47.1 us
    another operation x3, other arithmetic, shards(): jax.scipy.linalg.solve_triangular(lower_factor, sketch_part, lower=True)  39.4 us
    all_gather x1, waiting for transfers between devices, shards(): lax.all_gather(own_basis.astype(jnp.bfloat16), 'wide', axis=2, tiled=True)  38.7 us
    dot_general x1, matrix products, shards(): jnp.einsum('et,eib->tib', pick_target, contributions, precision=highest)  10.1 us
  transfers between devices with their start and end apart: 4, of which 4 were waited for; matrix products, arithmetic and copies ran while one was open for 0% of the time, Pallas kernels for 0%

commit v1 on v0

--- a/solution.py
+++ b/solution.py
@@ -3,6 +3,7 @@
 import jax.numpy as jnp
 from jax import lax
 from jax.sharding import PartitionSpec as P
+from jax.lax import all_gather
 
 
 def shards(entry_factor, entry_panel, entry_target, entry_count, panel_shared, coupling, probes):
@@ -37,7 +38,7 @@
     share_cols = full_width // wide_count
     sketch_part = lax.psum_scatter(sketch, "wide", scatter_dimension=2, tiled=True)
     gram_part = jnp.einsum("tib,tjb->tij", sketch_part, sketch_part, precision=highest)
-    gram_matrix = lax.psum(gram_part, "wide")
+    gram_matrix = jnp.sum(all_gather(gram_part, "wide"), axis=0)
     lower_factor = jnp.linalg.cholesky(gram_matrix)
     own_basis = jax.scipy.linalg.solve_triangular(lower_factor, sketch_part, lower=True)
     basis_round = lax.all_gather(own_basis.astype(jnp.bfloat16), "wide", axis=2, tiled=True)

time: 400 us -> 375 us (0.938)
  waiting for transfers between devices: 249 us -> 225 us
    psum x1 -> x0, waiting for transfers between devices: 71.6 us -> none  [shards(): gram_matrix = lax.psum(gram_part, 'wide')]
    all_gather x0 -> x1, waiting for transfers between devices: none -> 48.3 us  [shards(): gram_matrix = jnp.sum(all_gather(gram_part, 'wide'), axis=0)]
where the time goes in v1:
time: 375 us; the launch traced here: 374 us
  waiting for transfers between devices  225 us (60%)
  other arithmetic  91.4 us (24%)
  matrix products  34 us (9%)
  between operations  14.6 us (4%)
  blocking collectives  7.42 us (2%)
    reduce_scatter x1, waiting for transfers between devices, shards(): lax.psum_scatter(sketch, 'wide', scatter_dimension=2, tiled=True)  70.3 us
    reduce_scatter x1, waiting for transfers between devices, shards(): lax.psum_scatter(partial_rows, 'wide', scatter_dimension=2, tiled=True)  68 us
    all_gather x1, waiting for transfers between devices, shards(): gram_matrix = jnp.sum(all_gather(gram_part, 'wide'), axis=0)  48.3 us
    another operation x4, other arithmetic, shards(): lower_factor = jnp.linalg.cholesky(gram_matrix)  47.1 us
    another operation x3, other arithmetic, shards(): jax.scipy.linalg.solve_triangular(lower_factor, sketch_part, lower=True)  39.4 us
    all_gather x1, waiting for transfers between devices, shards(): lax.all_gather(own_basis.astype(jnp.bfloat16), 'wide', axis=2, tiled=True)  38 us
    dot_general x1, matrix products, shards(): jnp.einsum('et,eib->tib', pick_target, contributions, precision=highest)  10.1 us
  transfers between devices with their start and end apart: 4, of which 4 were waited for; matrix products, arithmetic and copies ran while one was open for 0% of the time, Pallas kernels for 0%

profile of v1, /device:TPU:0, one launch (start us, length us, event | category | flops | bytes accessed | tf_op | source)
XLA Modules:
  0.0 374.2 jit_solution(17686704222890137244)
XLA Ops:
  7.2 0.0 copy-start
  7.2 0.0 reduce-scatter.3.cloned.1.call-start
  7.2 0.7 fusion.36
  8.0 7.4 %all_gather.12 = bf16[2,64,1024]{2,1,0:T(8,128)(2,1)S(1)} all-gather(bf16[2,64,256]{2,1,0:T(8,128)(2,1)} %param.11), channel_id=1, replica_groups=mesh['wide'=8,'narrow'=4] {'narrow'}, dimensions={2}, use_global_device_ids=true | all-gather | bytes 327680 | tf_op jit(solution)/shard_map/all_gather | solution.py:25
  15.4 0.0 copy-done
  15.4 0.0 copy-start.2
  15.4 0.5 convolution_bitcast_fusion.1
  15.9 0.2 copy-done.2
  16.1 1.4 fusion.14
  17.5 0.2 copy.33
  17.7 0.3 reshape.98
  18.7 0.7 compare_select_fusion
  19.3 0.3 convolution_convert_fusion
  19.6 0.6 reshape.99
  20.2 0.0 copy-start.3
  20.3 3.8 %fusion.4 = f32[36,64,1024]{2,1,0:T(8,128)S(1)} fusion(bf16[36,64,64]{2,1,0:T(8,128)(2,1)S(1)} %reshape.99, bf16[36,1,64,1024]{3,2,1,0:T(8,128)(2,1)} %param.7), kind=kOutput, calls=%fused_computation.4 | convolution fusion | flops 301989888 | bytes 14450688 | tf_op jit(solution)/shard_map/eji,ejb->eib/dot_general | solution.py:35
  24.0 0.0 copy-done.3
  24.0 10.1 %fusion = f32[8,64,1024]{2,0,1:T(8,128)} fusion(f32[36,64,1024]{2,1,0:T(8,128)S(1)} %fusion.4, s32[36]{0:T(128)S(1)} %bitcast.80), kind=kOutput, calls=%fused_computation | convolution fusion | flops 226492704 | bytes 11534480 | tf_op jit(solution)/shard_map/et,eib->tib/dot_general | solution.py:36
  34.2 0.0 reduce-scatter.3.cloned.1.call-update
  34.2 0.0 all-gather.6.cloned.1.call-start
  34.2 70.3 %reduce-scatter.3.cloned.1.call-done = f32[8,64,128]{2,0,1:T(8,128)} async-done(((f32[8,64,1024]{2,0,1:T(8,128)}), f32[8,64,128]{2,0,1:T(8,128)}) %reduce-scatter.3.cloned.1.call-update) | async-done | bytes 262160 | tf_op jit(solution)/shard_map/reduce_scatter | solution.py:39
  104.5 0.0 copy-start.1
  104.5 2.4 fusion.25
  106.9 0.0 all-gather.6.cloned.1.call-update
  106.9 0.0 all-gather.4.cloned.1.call-start
  107.0 48.3 %all-gather.6.cloned.1.call-done = f32[64,64,64]{2,1,0:T(8,128)} async-done(((f32[8,64,64]{2,1,0:T(8,128)}), f32[64,64,64]{2,1,0:T(8,128)}) %all-gather.6.cloned.1.call-update) | async-done | bytes 1048592 | tf_op jit(solution)/shard_map/all_gather | solution.py:41
  155.3 1.8 reduce_sum.9
  157.2 0.1 copy.38
  157.3 46.9 %custom-call.8 = f32[8,64,64]{2,1,0:T(8,128)S(1)} custom-call(f32[8,64,64]{2,1,0:T(8,128)S(1)} %fusion.22), custom_call_target="Cholesky" | custom-call | tf_op jit(solution)/shard_map/jit(cholesky)/cholesky | solution.py:42
  204.3 0.1 compare_reduce_fusion
  204.4 0.1 select_bitcast_fusion
  204.5 39.3 %custom-call.9 = f32[8,1,64,64]{2,3,1,0:T(8,128)S(1)} custom-call(f32[8,1,64,64]{3,2,1,0:T(8,128)S(1)} %select_bitcast_fusion), custom_call_target="InvertDiagBlocksLowerTriangular" | custom-call | tf_op jit(solution)/shard_map/jit(_solve_triangular)/vmap()/triangular_solve | solution.py:43
  243.8 0.0 copy-done.1
  243.9 1.3 fusion.42
  245.2 0.0 all-gather.4.cloned.1.call-update
  245.2 0.0 reduce-scatter.5.cloned.1.call-start
  245.3 38.0 %all-gather.4.cloned.1.call-done = bf16[8,64,1024]{2,1,0:T(8,128)(2,1)} async-done(((bf16[8,64,128]{2,1,0:T(8,128)(2,1)}), bf16[8,64,1024]{2,1,0:T(8,128)(2,1)}) %all-gather.4.cloned.1.call-update) | async-done | bytes 1048592 | tf_op jit(solution)/shard_map/all_gather | solution.py:44
  283.3 2.8 convolution_convert_fusion.1
  286.1 5.5 %fusion.7 = f32[36,64,64]{1,2,0:T(8,128)S(1)} fusion(bf16[36,1,64,1024]{3,2,1,0:T(8,128)(2,1)} %param.7, bf16[36,64,1024]{2,0,1:T(8,128)(2,1)S(1)} %convolution_convert_fusion.1), kind=kOutput, calls=%fused_computation.10 | convolution fusion | flops 301989888 | bytes 10027008 | tf_op jit(solution)/shard_map/eib,ekb->eik/dot_general | solution.py:52
  291.6 0.5 copy.43
  292.1 0.8 fusion.12
  292.8 1.8 fusion.17
  294.7 3.3 convolution_bitcast_fusion
  298.0 0.0 reduce-scatter.5.cloned.1.call-update
  298.0 68.0 %reduce-scatter.5.cloned.1.call-done = f32[8,64,128]{2,1,0:T(8,128)} async-done(((f32[8,64,1024]{2,1,0:T(8,128)}), f32[8,64,128]{2,1,0:T(8,128)}) %reduce-scatter.5.cloned.1.call-update) | async-done | bytes 262160 | tf_op jit(solution)/shard_map/reduce_scatter | solution.py:59
  366.0 1.7 broadcast_multiply_fusion
  (5 shorter events, 0.1 us)
Async XLA Ops:
  7.2 8.2 %copy-start = (bf16[8,64,1024]{2,1,0:T(8,128)(2,1)S(1)}, bf16[8,64,1024]{2,1,0:T(8,128)(2,1)}, u32[]{:S(2)}) copy-start(bf16[8,64,1024]{2,1,0:T(8,128)(2,1)} %param.13) | copy-start | bytes 3145732
  7.2 97.3 %reduce-scatter.3.cloned.1.call-start = ((), (), s32[]{:S(2)}) async-start(), calls=%async_computation.2 | async-start | bytes 2359296 | tf_op jit(solution)/shard_map/reduce_scatter | solution.py:39
  15.4 0.7 copy-start.2
  20.2 3.8 %copy-start.3 = (s32[36,1]{0,1:T(1,128)S(1)}, s32[36,1]{0,1:T(1,128)}, u32[]{:S(2)}) copy-start(s32[36,1]{0,1:T(1,128)} %param.9) | copy-start | bytes 436
  34.2 121.1 %all-gather.6.cloned.1.call-start = ((), (), s32[]{:S(2)}) async-start(), calls=%async_computation.5 | async-start | bytes 2359296 | tf_op jit(solution)/shard_map/all_gather | solution.py:41
  104.5 139.3 %copy-start.1 = (f32[8,64,128]{2,0,1:T(8,128)S(1)}, f32[8,64,128]{2,0,1:T(8,128)}, u32[]{:S(2)}) copy-start(f32[8,64,128]{2,0,1:T(8,128)} %reduce-scatter.3.cloned.1.call-done) | copy-start | bytes 786436
  106.9 176.4 %all-gather.4.cloned.1.call-start = ((), (), s32[]{:S(2)}) async-start(), calls=%async_computation.3 | async-start | bytes 1179648 | tf_op jit(solution)/shard_map/all_gather | solution.py:44
  245.2 120.8 %reduce-scatter.5.cloned.1.call-start = ((), (), s32[]{:S(2)}) async-start(), calls=%async_computation.4 | async-start | bytes 2359296 | tf_op jit(solution)/shard_map/reduce_scatter | solution.py:59
Sparse Core Ops, SparseCore 0:
  34.3 70.1 reduce-scatter.2
  107.2 48.0 all-gather.5
  245.3 37.9 all-gather.3
  298.1 67.8 reduce-scatter.4
